TPU v7x, 256 devices: a whole 4x4x8 slice. The times are simulated.
256 devices in a mesh: af: 64 (over y_hi, z, x), row: 4 (over y_lo, core).
Axes of the slice: x: 4, y: 4 (y_hi: 2, y_lo: 2; y = y_hi * 2 + y_lo), z: 8, core: 2. Of those that a mesh axis runs over, the one named last changes fastest.
Arguments:
- source_traces: bfloat16 [512, 1024, 2048], P('af', 'row'), may hold values from -6 to 6
- receiver_traces: bfloat16 [128, 1024, 2048], P('row', 'af'), may hold values from -6 to 6
- wavelet_inverse: float32 [64, 2], replicated, may hold values from -4 to 4
Outputs:
- multiples: bfloat16 [512, 128, 2048], P('af', 'row')
All inputs are finite; a program needn't handle non-finite values.
Results may differ from a plain program's by a relative error of at most 0.008.
Values may be sent and summed in bfloat16 or wider, within the bound.
No kernel may reach another device: no remote copies, remote signals or barrier semaphores. Data moves between devices by JAX's collectives and lax.ppermute only.
A program may use at most 64 MiB of HBM per device.

v0:
```python
import math
import jax
import jax.numpy as jnp
from jax import lax
from jax.sharding import PartitionSpec as P

NT = 2048
NF = 64
F_LOW = 96
K = 1024


def tables(amplitude):
    samples = jnp.arange(NT, dtype=jnp.int32)
    frequency = F_LOW + jnp.arange(NF, dtype=jnp.int32)
    phase_index = frequency[:, None] * samples[None, :] % NT
    angles = phase_index.astype(jnp.float32) * (2.0 * math.pi / NT)
    return jnp.stack([jnp.cos(angles) * amplitude, -jnp.sin(angles) * amplitude], axis=1).astype(
        jnp.bfloat16
    )


def coupling(recv_block):
    rcv_real = recv_block[:, 0]
    rcv_imag = recv_block[:, 1]
    real_row = jnp.stack([rcv_real, -rcv_imag], axis=1)
    imag_row = jnp.stack([rcv_imag, rcv_real], axis=1)
    return jnp.stack([real_row, imag_row], axis=1)


def per_device(source_traces, receiver_traces, wavelet_inverse):
    forward = tables(1.0 / math.sqrt(NT))
    source_spec = jnp.einsum(
        "fct,skt->fcsk", forward, source_traces, preferred_element_type=jnp.float32
    ).astype(jnp.bfloat16)
    receiver_spec = jnp.einsum(
        "fct,rkt->fckr", forward, receiver_traces, preferred_element_type=jnp.float32
    ).astype(jnp.bfloat16)
    source_freq, receiver_freq = (
        lax.all_to_all(source_spec, "af", split_axis=0, concat_axis=2, tiled=True),
        lax.all_to_all(receiver_spec, "af", split_axis=0, concat_axis=2, tiled=True),
    )
    local_freqs = source_freq.shape[0]
    raw = jnp.einsum(
        "fockr,fcsk->rfos",
        coupling(receiver_freq),
        lax.all_gather(source_freq, "row", axis=3, tiled=True),
        preferred_element_type=jnp.float32,
    )
    first_freq = lax.axis_index("af") * local_freqs
    wavelet_rows = lax.dynamic_slice_in_dim(wavelet_inverse, first_freq, local_freqs, 0)
    wave_real = wavelet_rows[:, 0][None, :, None]
    wave_imag = wavelet_rows[:, 1][None, :, None]
    raw_real = raw[:, :, 0, :]
    raw_imag = raw[:, :, 1, :]
    amplitude = 1.0 / math.sqrt(K)
    pred_real = (raw_real * wave_real - raw_imag * wave_imag) * amplitude
    pred_imag = (raw_real * wave_imag + raw_imag * wave_real) * amplitude
    predicted = jnp.stack([pred_real, pred_imag], axis=2).astype(jnp.bfloat16)
    returned = lax.all_to_all(predicted, "af", split_axis=3, concat_axis=1, tiled=True)
    inverse = tables(1.0 / math.sqrt(NF))
    result = jnp.einsum("rfcs,fct->srt", returned, inverse, preferred_element_type=jnp.float32)
    return result.astype(jnp.bfloat16)


def solution(mesh):
    return jax.shard_map(
        per_device,
        mesh=mesh,
        in_specs=(P("af", "row", None), P("row", "af", None), P()),
        out_specs=P("af", "row", None),
        check_vma=False,
    )
```

profile of v0, /device:TPU:1, one launch (start us, length us, event | category | flops | bytes accessed | tf_op | source)
XLA Modules:
  0.0 115.3 jit_solution(388761204805325706)
XLA Ops:
  6.5 2.5 %multiply_convert_fusion.1 = (bf16[64,1,2048]{2,0,1:T(8,128)(2,1)S(1)}, bf16[64,1,2048]{2,0,1:T(8,128)(2,1)S(1)}, bf16[64,1,2048]{2,0,1:T(8,128)(2,1)S(1)}, bf16[64,1,2048]{2,0,1:T(8,128)(2,1)S(1)}) fusion(s32[64]{0:T(128)S(1)} %iota_add_fusion), kind=kLoop, calls=%fused_computation.26 | loop fusion | flops 3014656 | bytes 1048832 | tf_op jit(solution)/shard_map/convert.2
  9.1 6.3 %fusion.9 = bf16[64,2,8,256]{3,0,2,1:T(8,128)(2,1)S(1)} fusion(bf16[8,256,2048]{2,1,0:T(8,128)(2,1)} %param.3, bf16[64,1,2048]{2,0,1:T(8,128)(2,1)S(1)} %get-tuple-element.15, bf16[64,1,2048]{2,0,1:T(8,128)(2,1)S(1)} %get-tuple-element.13), kind=kOutput, calls=%fused_computation.10 | convolution fusion | flops 1075052544 | bytes 9437184 | tf_op jit(solution)/shard_map/fct,skt->fcsk/dot_general | solution.py:33
  15.3 0.3 copy.13
  15.6 32.5 %all_to_all.54 = bf16[64,2,8,256]{3,2,1,0:T(8,128)(2,1)S(1)} all-to-all(bf16[64,2,8,256]{3,2,1,0:T(8,128)(2,1)S(1)} %copy.13), channel_id=1, replica_groups=mesh['af'=64,'row'=4] {'af'}, dimensions={0} | all-to-all | bytes 1048576 | tf_op jit(solution)/shard_map/all_to_all | solution.py:40
  48.1 0.8 copy.39
  49.0 1.5 %fusion.15 = bf16[64,2,16,32]{0,3,2,1:T(8,128)(2,1)S(1)} fusion(bf16[32,16,2048]{2,1,0:T(8,128)(2,1)S(1)} %copy-done.1, bf16[64,1,2048]{2,0,1:T(8,128)(2,1)S(1)} %get-tuple-element.15, bf16[64,1,2048]{2,0,1:T(8,128)(2,1)S(1)} %get-tuple-element.13), kind=kOutput, calls=%fused_computation.12 | convolution fusion | flops 269549568 | bytes 2752512 | tf_op jit(solution)/shard_map/fct,rkt->fckr/dot_general | solution.py:36
  50.5 0.8 copy.16
  51.3 1.1 reshape.223
  52.4 6.9 %all-to-all-start.1 = ((bf16[64,2,512]{2,1,0:T(2,128)(2,1)}), bf16[64,2,512]{2,1,0:T(2,128)(2,1)S(1)}, u32[]{:S(2)}, u32[]{:S(2)}) async-start(bf16[64,2,512]{2,1,0:T(2,128)(2,1)} %reshape.223), calls=%async_computation.1 | async-start | bytes 262144 | tf_op jit(solution)/shard_map/all_to_all | solution.py:41
  59.3 0.1 constant_dynamic-slice_fusion
  59.4 0.6 fusion.38
  60.0 10.8 %all-to-all-done.1 = bf16[64,2,512]{2,1,0:T(2,128)(2,1)S(1)} async-done(((bf16[64,2,512]{2,1,0:T(2,128)(2,1)}), bf16[64,2,512]{2,1,0:T(2,128)(2,1)S(1)}, u32[]{:S(2)}, u32[]{:S(2)}) %all-to-all-start.1) | async-done | bytes 131104 | tf_op jit(solution)/shard_map/all_to_all | solution.py:41
  70.8 0.3 reshape.224
  71.2 0.1 copy.29
  71.3 0.1 copy.28
  71.5 7.5 %all-gather.2.cloned.1.call-done = bf16[1,2,512,1024]{3,2,1,0:T(8,128)(2,1)} async-done(((bf16[1,2,512,256]{3,2,1,0:T(8,128)(2,1)}), bf16[1,2,512,1024]{3,2,1,0:T(8,128)(2,1)}) %all-gather.2.cloned.1.call-update) | async-done | bytes 2097168 | tf_op jit(solution)/shard_map/all_gather | solution.py:47
  79.0 2.4 %fusion.18 = f32[32,1,2,512]{3,0,2,1:T(8,128)S(1)} fusion(bf16[1,2,512,1024]{3,2,1,0:T(8,128)(2,1)} %all-gather.2.cloned.1.call-done, bf16[1,1,2,1024,32]{3,4,2,1,0:T(8,128)(2,1)S(1)} %get-tuple-element.10, bf16[1,1,2,1024,32]{3,4,2,1,0:T(8,128)(2,1)S(1)} %get-tuple-element.9), kind=kOutput, calls=%fused_computation.13 | convolution fusion | flops 134742016 | bytes 2490368 | tf_op jit(solution)/shard_map/fockr,fcsk->rfos/dot_general | solution.py:44
  81.4 1.3 %multiply_convert_fusion.5 = (bf16[32,1,1,512]{3,0,2,1:T(8,128)(2,1)S(1)}, bf16[32,1,1,512]{3,0,2,1:T(8,128)(2,1)S(1)}) fusion(f32[32,1,2,512]{3,0,2,1:T(8,128)S(1)} %fusion.18, f32[]{:T(128)} %bitcast.24, f32[]{:T(128)} %bitcast.22), kind=kLoop, calls=%fused_computation.42 | loop fusion | flops 163840 | bytes 196616 | tf_op jit(solution)/shard_map/convert
  82.6 0.2 copy.20
  82.8 0.2 reshape.225
  83.0 23.5 %all_to_all.55 = bf16[64,2,256]{2,1,0:T(2,128)(2,1)S(1)} all-to-all(bf16[64,2,256]{2,1,0:T(2,128)(2,1)S(1)} %reshape.225), channel_id=1, replica_groups=mesh['af'=64,'row'=4] {'af'}, dimensions={0} | all-to-all | bytes 131072 | tf_op jit(solution)/shard_map/all_to_all | solution.py:60
  106.5 0.2 reshape.226
  106.7 0.3 copy.22
  107.0 1.4 %fusion.3 = bf16[8,32,2048]{2,1,0:T(8,128)(2,1)} fusion(bf16[64,1,2048]{2,0,1:T(8,128)(2,1)S(1)} %get-tuple-element.14, bf16[64,1,2048]{2,0,1:T(8,128)(2,1)S(1)} %get-tuple-element.16, bf16[32,1,2,64,8]{3,0,2,4,1:T(8,128)(2,1)S(1)} %copy.22), kind=kOutput, calls=%fused_computation.4 | convolution fusion | flops 135790592 | bytes 1638400 | tf_op jit(solution)/shard_map/rfcs,fct->srt/dot_general | solution.py:62
  (12 shorter events, 0.2 us)
Async XLA Ops:
  6.5 52.8 %copy-start = (f32[64,2]{0,1:T(2,128)S(1)}, f32[64,2]{0,1:T(2,128)}, u32[]{:S(2)}) copy-start(f32[64,2]{0,1:T(2,128)} %param.5) | copy-start | bytes 1540
  6.5 72.5 %all-gather.2.cloned.1.call-start = ((), (), s32[]{:S(2)}) async-start(), calls=%async_computation.3 | async-start | bytes 2621440 | tf_op jit(solution)/shard_map/all_gather | solution.py:47
  15.3 33.7 %copy-start.1 = (bf16[32,16,2048]{2,1,0:T(8,128)(2,1)S(1)}, bf16[32,16,2048]{2,1,0:T(8,128)(2,1)}, u32[]{:S(2)}) copy-start(bf16[32,16,2048]{2,1,0:T(8,128)(2,1)} %param.4) | copy-start | bytes 6291460
  52.4 18.4 %all-to-all-start.1 = ((bf16[64,2,512]{2,1,0:T(2,128)(2,1)}), bf16[64,2,512]{2,1,0:T(2,128)(2,1)S(1)}, u32[]{:S(2)}, u32[]{:S(2)}) async-start(bf16[64,2,512]{2,1,0:T(2,128)(2,1)} %reshape.223), calls=%async_computation.1 | async-start | bytes 262144 | tf_op jit(solution)/shard_map/all_to_all | solution.py:41
Sparse Core Ops, SparseCore 0:
  49.1 29.8 all-gather.1
where the time goes:
time: 116 us; the launch traced here: 115 us
  blocking collectives  56 us (48%)
  waiting for transfers between devices  18.3 us (16%)
  between operations  13.5 us (12%)
  matrix products  11.6 us (10%)
  starting transfers between devices  6.93 us (6%)
  local copies, waits for them, and re-layouts  5.02 us (4%)
  other arithmetic  3.83 us (3%)
    all_to_all x1, blocking collectives, per_device(): lax.all_to_all(source_spec, 'af', split_axis=0, concat_axis=2, tiled=True)  32.5 us
    all_to_all x1, blocking collectives, per_device(): lax.all_to_all(predicted, 'af', split_axis=3, concat_axis=1, tiled=True)  23.5 us
    all_to_all x1, waiting for transfers between devices, per_device(): lax.all_to_all(receiver_spec, 'af', split_axis=0, concat_axis=2, tiled=True)  10.8 us
    all_gather x1, waiting for transfers between devices, per_device(): lax.all_gather(source_freq, 'row', axis=3, tiled=True)  7.53 us
    all_to_all x1, starting transfers between devices, per_device(): lax.all_to_all(receiver_spec, 'af', split_axis=0, concat_axis=2, tiled=True)  6.92 us
    dot_general x1, matrix products, per_device(): jnp.einsum('fct,skt->fcsk', forward, source_traces, preferred_element_typ...  6.26 us
    another operation x2, other arithmetic  3.78 us
    dot_general x1, matrix products, per_device(): jnp.einsum('fockr,fcsk->rfos', coupling(receiver_freq), lax.all_gather(so...  2.35 us
  transfers between devices with their start and end apart: 2, of which 2 were waited for; matrix products, arithmetic and copies ran while one was open for 4% of the time, Pallas kernels for 0%

commit v1 on v0

--- a/solution.py
+++ b/solution.py
@@ -8,6 +8,12 @@
 NF = 64
 F_LOW = 96
 K = 1024
+
+
+def _connect_halves(payload, dim_i):
+    return jnp.concatenate(
+        lax.all_to_all(jnp.stack(lax.axis_size("row") * [payload], 0), "row", 0, 0), dim_i
+    )
 
 
 def tables(amplitude):
@@ -44,7 +50,7 @@
     raw = jnp.einsum(
         "fockr,fcsk->rfos",
         coupling(receiver_freq),
-        lax.all_gather(source_freq, "row", axis=3, tiled=True),
+        _connect_halves(source_freq, 3),
         preferred_element_type=jnp.float32,
     )
     first_freq = lax.axis_index("af") * local_freqs

time: 116 us -> 120 us (1.034)
  blocking collectives: 56 us -> 14.9 us
  waiting for transfers between devices: 18.3 us -> 47.4 us
  starting transfers between devices: 6.93 us -> 28.5 us
  between operations: 13.5 us -> 0.15 us
  local copies, waits for them, and re-layouts: 5.02 us -> 12.6 us
    all_to_all x0 -> x2, waiting for transfers between devices: none -> 36 us  [the longest x1 23.5 us: _connect_halves(): lax.all_to_all(jnp.stack(lax.axis_size('row') * [payload], 0), 'row', 0, 0)]
    all_to_all x1 -> x0, blocking collectives: 32.5 us -> none  [per_device(): lax.all_to_all(source_spec, 'af', split_axis=0, concat_axis=2, tiled=True)]
    all_to_all x0 -> x2, starting transfers between devices: none -> 21.6 us  [the longest x1 15.1 us: per_device(): lax.all_to_all(source_spec, 'af', split_axis=0, concat_axis=2, tiled=True)]
    all_to_all x1, blocking collectives: 23.5 us -> 14.9 us  [per_device(): lax.all_to_all(predicted, 'af', split_axis=3, concat_axis=1, tiled=True)]
    all_gather x1 -> x0, waiting for transfers between devices: 7.53 us -> none  [per_device(): lax.all_gather(source_freq, 'row', axis=3, tiled=True)]
    another operation x0 -> x2, local copies, waits for them, and re-layouts: none -> 4.7 us
    reshape x0 -> x1, local copies, waits for them, and re-layouts: none -> 2.95 us  [_connect_halves(): jnp.concatenate(lax.all_to_all(jnp.stack(lax.axis_size('row') * [payload]...]
    dot_general x1, matrix products: 2.35 us -> 0.76 us  [per_device(): jnp.einsum('fockr,fcsk->rfos', coupling(receiver_freq), _connect_halves(s...]
  transfers between devices with their start and end apart: 2 -> 3, of which waited for: 2 -> 3; matrix products, arithmetic and copies ran while one was open for 4% -> 5% of each run, Pallas kernels for 0% -> 0%
where the time goes in v1:
time: 120 us; the launch traced here: 119 us
  waiting for transfers between devices  47.4 us (40%)
  starting transfers between devices  28.5 us (24%)
  blocking collectives  14.9 us (12%)
  local copies, waits for them, and re-layouts  12.6 us (10%)
  matrix products  11.5 us (10%)
  other arithmetic  3.93 us (3%)
    all_to_all x1, waiting for transfers between devices, _connect_halves(): lax.all_to_all(jnp.stack(lax.axis_size('row') * [payload], 0), 'row', 0, 0)  23.5 us
    all_to_all x1, starting transfers between devices, per_device(): lax.all_to_all(source_spec, 'af', split_axis=0, concat_axis=2, tiled=True)  15.1 us
    all_to_all x1, blocking collectives, per_device(): lax.all_to_all(predicted, 'af', split_axis=3, concat_axis=1, tiled=True)  14.9 us
    all_to_all x1, waiting for transfers between devices, per_device(): lax.all_to_all(source_spec, 'af', split_axis=0, concat_axis=2, tiled=True)  12.5 us
    all_to_all x1, waiting for transfers between devices, per_device(): lax.all_to_all(receiver_spec, 'af', split_axis=0, concat_axis=2, tiled=True)  11.4 us
    all_to_all x1, starting transfers between devices, per_device(): lax.all_to_all(receiver_spec, 'af', split_axis=0, concat_axis=2, tiled=True)  6.92 us
    all_to_all x1, starting transfers between devices, _connect_halves(): lax.all_to_all(jnp.stack(lax.axis_size('row') * [payload], 0), 'row', 0, 0)  6.48 us
    dot_general x1, matrix products, per_device(): jnp.einsum('fct,skt->fcsk', forward, source_traces, preferred_element_typ...  6.26 us
  transfers between devices with their start and end apart: 3, of which 3 were waited for; matrix products, arithmetic and copies ran while one was open for 5% of the time, Pallas kernels for 0%

profile of v1, /device:TPU:1, one launch (start us, length us, event | category | flops | bytes accessed | tf_op | source)
XLA Modules:
  0.0 119.1 jit_solution(17414040502436916811)
XLA Ops:
  0.0 2.5 %multiply_convert_fusion.1 = (bf16[64,1,2048]{2,0,1:T(8,128)(2,1)S(1)}, bf16[64,1,2048]{2,0,1:T(8,128)(2,1)S(1)}, bf16[64,1,2048]{2,0,1:T(8,128)(2,1)S(1)}, bf16[64,1,2048]{2,0,1:T(8,128)(2,1)S(1)}) fusion(s32[64]{0:T(128)S(1)} %iota_add_fusion), kind=kLoop, calls=%fused_computation.24 | loop fusion | flops 3014656 | bytes 1048832 | tf_op jit(solution)/shard_map/convert.2
  2.5 6.3 %fusion.7 = bf16[64,2,8,256]{3,0,2,1:T(8,128)(2,1)S(1)} fusion(bf16[8,256,2048]{2,1,0:T(8,128)(2,1)} %param.3, bf16[64,1,2048]{2,0,1:T(8,128)(2,1)S(1)} %get-tuple-element.15, bf16[64,1,2048]{2,0,1:T(8,128)(2,1)S(1)} %get-tuple-element.13), kind=kOutput, calls=%fused_computation.8 | convolution fusion | flops 1075052544 | bytes 9437184 | tf_op jit(solution)/shard_map/fct,skt->fcsk/dot_general | solution.py:39
  8.8 1.1 copy.13
  9.9 15.1 %all-to-all-start = ((bf16[64,2,8,256]{3,2,1,0:T(8,128)(2,1)}), bf16[64,2,8,256]{3,2,1,0:T(8,128)(2,1)S(1)}, u32[]{:S(2)}, u32[]{:S(2)}) async-start(bf16[64,2,8,256]{3,2,1,0:T(8,128)(2,1)} %copy.13), calls=%async_computation | async-start | bytes 1048576 | tf_op jit(solution)/shard_map/all_to_all | solution.py:46
  25.0 3.1 %fusion.13 = bf16[64,2,16,32]{0,3,2,1:T(8,128)(2,1)S(1)} fusion(bf16[32,16,2048]{2,1,0:T(8,128)(2,1)} %param.4, bf16[64,1,2048]{2,0,1:T(8,128)(2,1)S(1)} %get-tuple-element.15, bf16[64,1,2048]{2,0,1:T(8,128)(2,1)S(1)} %get-tuple-element.13), kind=kOutput, calls=%fused_computation.10 | convolution fusion | flops 269549568 | bytes 2752512 | tf_op jit(solution)/shard_map/fct,rkt->fckr/dot_general | solution.py:42
  28.1 0.8 copy.17
  28.9 1.1 reshape.235
  29.9 12.5 %all-to-all-done = bf16[64,2,8,256]{3,2,1,0:T(8,128)(2,1)S(1)} async-done(((bf16[64,2,8,256]{3,2,1,0:T(8,128)(2,1)}), bf16[64,2,8,256]{3,2,1,0:T(8,128)(2,1)S(1)}, u32[]{:S(2)}, u32[]{:S(2)}) %all-to-all-start) | async-done | bytes 524320 | tf_op jit(solution)/shard_map/all_to_all | solution.py:46
  42.5 6.9 %all-to-all-start.2 = ((bf16[64,2,512]{2,1,0:T(2,128)(2,1)}), bf16[64,2,512]{2,1,0:T(2,128)(2,1)S(1)}, u32[]{:S(2)}, u32[]{:S(2)}) async-start(bf16[64,2,512]{2,1,0:T(2,128)(2,1)} %reshape.235), calls=%async_computation.2 | async-start | bytes 262144 | tf_op jit(solution)/shard_map/all_to_all | solution.py:47
  49.4 11.4 %all-to-all-done.2 = bf16[64,2,512]{2,1,0:T(2,128)(2,1)S(1)} async-done(((bf16[64,2,512]{2,1,0:T(2,128)(2,1)}), bf16[64,2,512]{2,1,0:T(2,128)(2,1)S(1)}, u32[]{:S(2)}, u32[]{:S(2)}) %all-to-all-start.2) | async-done | bytes 131104 | tf_op jit(solution)/shard_map/all_to_all | solution.py:47
  60.9 1.5 %stack.45 = bf16[4,1,2,512,256]{4,3,2,1,0:T(8,128)(2,1)} broadcast(bf16[2,512,256]{2,1,0:T(8,128)(2,1)S(1)} %bitcast.69), dimensions={2,3,4} | broadcast | bytes 2621440 | tf_op jit(solution)/shard_map/stack | solution.py:15
  62.3 6.5 %all-to-all-start.1 = ((bf16[4,1,2,512,256]{4,3,2,1,0:T(8,128)(2,1)}), bf16[4,1,2,512,256]{4,3,2,1,0:T(8,128)(2,1)S(1)}, u32[]{:S(2)}, u32[]{:S(2)}) async-start(bf16[4,1,2,512,256]{4,3,2,1,0:T(8,128)(2,1)} %stack.45), calls=%async_computation.1 | async-start | bytes 4194304 | tf_op jit(solution)/shard_map/all_to_all | solution.py:15
  68.9 0.6 fusion.33
  69.5 0.3 reshape.236
  70.1 23.5 %all-to-all-done.1 = bf16[4,1,2,512,256]{4,3,2,1,0:T(8,128)(2,1)S(1)} async-done(((bf16[4,1,2,512,256]{4,3,2,1,0:T(8,128)(2,1)}), bf16[4,1,2,512,256]{4,3,2,1,0:T(8,128)(2,1)S(1)}, u32[]{:S(2)}, u32[]{:S(2)}) %all-to-all-start.1) | async-done | bytes 2097184 | tf_op jit(solution)/shard_map/all_to_all | solution.py:15
  93.6 2.9 %copy.15 = bf16[1,2,512,4,256]{4,3,2,1,0:T(4,128)(2,1)} copy(bf16[1,2,512,4,256]{4,2,1,0,3:T(8,128)(2,1)S(1)} %bitcast.68) | data formatting | bytes 4194304 | tf_op jit(solution)/shard_map/reshape | solution.py:14
  96.6 3.2 %reshape.230 = bf16[2,512,1024,1]{2,1,0,3:T(8,128)(2,1)S(1)} reshape(bf16[1,2,512,4,256]{4,3,2,1,0:T(4,128)(2,1)} %copy.15) | data formatting | bytes 4194304 | tf_op jit(solution)/shard_map/reshape.4
  99.8 0.8 convolution_bitcast_fusion.1
  100.6 1.3 %multiply_convert_fusion.5 = (bf16[32,1,1,512]{3,0,2,1:T(8,128)(2,1)S(1)}, bf16[32,1,1,512]{3,0,2,1:T(8,128)(2,1)S(1)}) fusion(f32[32,1,2,512]{3,0,2,1:T(8,128)S(1)} %convolution_bitcast_fusion.1, f32[]{:T(128)} %bitcast.23, f32[]{:T(128)} %bitcast.21), kind=kLoop, calls=%fused_computation.40 | loop fusion | flops 163840 | bytes 196616 | tf_op jit(solution)/shard_map/convert
  102.1 0.2 reshape.237
  102.3 14.9 %all_to_all.56 = bf16[64,2,256]{2,1,0:T(2,128)(2,1)S(1)} all-to-all(bf16[64,2,256]{2,1,0:T(2,128)(2,1)S(1)} %reshape.237), channel_id=1, replica_groups=mesh['af'=64,'row'=4] {'af'}, dimensions={0} | all-to-all | bytes 131072 | tf_op jit(solution)/shard_map/all_to_all | solution.py:66
  117.2 0.2 reshape.238
  117.4 0.3 copy.23
  117.7 1.4 %fusion.3 = bf16[8,32,2048]{2,1,0:T(8,128)(2,1)} fusion(bf16[64,1,2048]{2,0,1:T(8,128)(2,1)S(1)} %get-tuple-element.14, bf16[64,1,2048]{2,0,1:T(8,128)(2,1)S(1)} %get-tuple-element.16, bf16[32,1,2,64,8]{3,0,2,4,1:T(8,128)(2,1)S(1)} %copy.23), kind=kOutput, calls=%fused_computation.4 | convolution fusion | flops 135790592 | bytes 1638400 | tf_op jit(solution)/shard_map/rfcs,fct->srt/dot_general | solution.py:68
  (13 shorter events, 0.6 us)
Async XLA Ops:
  0.0 68.8 %copy-start = (f32[64,2]{0,1:T(2,128)S(1)}, f32[64,2]{0,1:T(2,128)}, u32[]{:S(2)}) copy-start(f32[64,2]{0,1:T(2,128)} %param.5) | copy-start | bytes 1540
  9.9 32.6 %all-to-all-start = ((bf16[64,2,8,256]{3,2,1,0:T(8,128)(2,1)}), bf16[64,2,8,256]{3,2,1,0:T(8,128)(2,1)S(1)}, u32[]{:S(2)}, u32[]{:S(2)}) async-start(bf16[64,2,8,256]{3,2,1,0:T(8,128)(2,1)} %copy.13), calls=%async_computation | async-start | bytes 1048576 | tf_op jit(solution)/shard_map/all_to_all | solution.py:46
  42.5 18.4 %all-to-all-start.2 = ((bf16[64,2,512]{2,1,0:T(2,128)(2,1)}), bf16[64,2,512]{2,1,0:T(2,128)(2,1)S(1)}, u32[]{:S(2)}, u32[]{:S(2)}) async-start(bf16[64,2,512]{2,1,0:T(2,128)(2,1)} %reshape.235), calls=%async_computation.2 | async-start | bytes 262144 | tf_op jit(solution)/shard_map/all_to_all | solution.py:47
  62.3 31.3 %all-to-all-start.1 = ((bf16[4,1,2,512,256]{4,3,2,1,0:T(8,128)(2,1)}), bf16[4,1,2,512,256]{4,3,2,1,0:T(8,128)(2,1)S(1)}, u32[]{:S(2)}, u32[]{:S(2)}) async-start(bf16[4,1,2,512,256]{4,3,2,1,0:T(8,128)(2,1)} %stack.45), calls=%async_computation.1 | async-start | bytes 4194304 | tf_op jit(solution)/shard_map/all_to_all | solution.py:15
